TPU v7x, 512 devices: a whole 4x8x8 slice. The times are simulated.
512 devices in a mesh: dom: 512 (over x, y, z, core).
Axes of the slice: x: 4, y: 8, z: 8, core: 2. Of those that a mesh axis runs over, the one named last changes fastest.
Arguments:
- features: bfloat16 [589824, 128], P('dom'), may hold values from -6 to 6
- targets: bfloat16 [589824, 128], P('dom'), may hold values from -6 to 6
- first_weight: bfloat16 [128, 128], replicated, may hold values from -0.5 to 0.5
- second_weight: bfloat16 [128, 128], replicated, may hold values from -0.5 to 0.5
- local_bonds: bfloat16 [589824, 1152], P('dom'), may hold values from -0.4375 to 0.4375
- halo_bonds: bfloat16 [589824, 512], P('dom'), may hold values from -0.4375 to 0.4375
- tile_mask: int32 [9216, 18], P('dom'), may hold values 0 or 1
- send_rows: int32 [2048, 128], P('dom'), may hold values from 0 to 1151
Outputs:
- prediction: bfloat16 [589824, 128], P('dom')
- grad_first: float32 [128, 128], replicated
- grad_second: float32 [128, 128], replicated
Inputs may be any that keep to these rules, and one draw needn't show every extreme that they name: `tile_mask`: tile presence flags. `send_rows`: local atom numbers of the sending partition; repeats allowed.
All inputs are finite; a program needn't handle non-finite values. No bound on the sum of `tile_mask` on one device may be relied on, other than what follows from the above.
Results may differ from a plain program's by a relative error of at most 0.004.
The roundings to bfloat16 on the way count: a program that leaves them out, or rounds other values in their place, can miss the bound.
Values may be sent and summed in bfloat16 or wider, within the bound.
A program may use at most 64 MiB of HBM per device.

v0:
```python
import math

import jax
import jax.numpy as jnp
from jax import lax
from jax.sharding import PartitionSpec as P

ROUNDS = 4


def swapped(value, axis, apart):
    mask = 2**apart
    pairs = [(source, source ^ mask) for source in range(lax.axis_size(axis))]
    return lax.ppermute(value, axis, pairs)


def spread_mask(tile_mask):
    return jnp.repeat(jnp.repeat(tile_mask, 64, axis=0), 64, axis=1).astype(jnp.bfloat16)


def contract_rows(left, right):
    return lax.dot_general(
        left, right, (((0,), (0,)), ((), ())), preferred_element_type=jnp.float32
    )


def fetch_inputs(rows, send_rows):
    pieces = []
    for turn in range(ROUNDS):
        chosen = jnp.take(rows, send_rows[turn], axis=0)
        pieces.append(swapped(chosen, "dom", turn))
    return jnp.concatenate(pieces, axis=0)


def fetch_hidden(rows, send_rows):
    pieces = []
    for turn in range(ROUNDS):
        chosen = jnp.take(rows, send_rows[turn], axis=0)
        pieces.append(swapped(chosen, "dom", turn))
    return jnp.concatenate(pieces, axis=0)


def return_grads(halo_cot, send_rows, row_count):
    width = send_rows.shape[1]
    total = jnp.zeros((row_count, halo_cot.shape[1]), jnp.float32)
    for turn in range(ROUNDS):
        block = halo_cot[turn * width : (turn + 1) * width]
        back = swapped(block.astype(jnp.bfloat16), "dom", turn).astype(block.dtype)
        total = total.at[send_rows[turn]].add(back)
    return total


def local(
    features, targets, first_weight, second_weight, local_bonds, halo_bonds, tile_mask, send_rows
):
    row_count = features.shape[0]
    bond_tiles = local_bonds * spread_mask(tile_mask)
    halo_inputs = fetch_inputs(features, send_rows)
    inner_first = jnp.dot(bond_tiles, features, preferred_element_type=jnp.float32)
    first_sum = inner_first + jnp.dot(halo_bonds, halo_inputs, preferred_element_type=jnp.float32)
    first_agg = first_sum.astype(jnp.bfloat16)
    first_pre = jnp.dot(first_agg, first_weight, preferred_element_type=jnp.float32)
    hidden = (features.astype(jnp.float32) + jax.nn.silu(first_pre)).astype(jnp.bfloat16)
    halo_hidden = fetch_hidden(hidden, send_rows)
    inner_second = jnp.dot(bond_tiles, hidden, preferred_element_type=jnp.float32)
    second_sum = inner_second + jnp.dot(halo_bonds, halo_hidden, preferred_element_type=jnp.float32)
    second_agg = second_sum.astype(jnp.bfloat16)
    output = hidden.astype(jnp.float32) + jnp.dot(
        second_agg, second_weight, preferred_element_type=jnp.float32
    )
    prediction = output.astype(jnp.bfloat16)
    scale = 1.0 / math.sqrt(row_count * lax.axis_size("dom"))
    error = (output - targets.astype(jnp.float32)) * scale
    error_b = error.astype(jnp.bfloat16)
    grad_second = contract_rows(second_agg, error_b)
    agg_cot = lax.dot_general(
        error_b, second_weight, (((1,), (1,)), ((), ())), preferred_element_type=jnp.float32
    ).astype(jnp.bfloat16)
    halo_cot = contract_rows(halo_bonds, agg_cot)
    returned = return_grads(halo_cot, send_rows, row_count)
    inner_cot = contract_rows(bond_tiles, agg_cot)
    hidden_cot = error + inner_cot + returned
    sigm = jax.nn.sigmoid(first_pre)
    pre_cot = (hidden_cot * sigm * (1.0 + first_pre * (1.0 - sigm))).astype(jnp.bfloat16)
    grad_first = contract_rows(first_agg, pre_cot)
    grad_first, grad_second = lax.psum((grad_first, grad_second), "dom")
    return (prediction, grad_first, grad_second)


def solution(mesh):
    in_specs = (
        P("dom", None),
        P("dom", None),
        P(),
        P(),
        P("dom", None),
        P("dom", None),
        P("dom", None),
        P("dom", None),
    )
    out_specs = (P("dom", None), P(), P())
    return jax.shard_map(local, mesh=mesh, in_specs=in_specs, out_specs=out_specs, check_vma=False)
```

profile of v0, /device:TPU:1, one launch (start us, length us, event | category | flops | bytes accessed | tf_op | source)
XLA Modules:
  0.0 366.6 jit_solution(3487240273709664590)
XLA Ops:
  7.2 0.0 copy-start
  7.2 0.0 all-reduce.3.cloned.1.call-start
  7.2 0.8 compare_and_fusion.3
  8.1 1.7 gather_fusion
  9.7 0.1 broadcast_select_fusion.7
  9.8 8.7 %collective-permute-start = (bf16[128,128]{1,0:T(8,128)(2,1)S(1)}, bf16[128,128]{1,0:T(8,128)(2,1)S(1)}, u32[]{:S(2)}, u32[]{:S(2)}) collective-permute-start(bf16[128,128]{1,0:T(8,128)(2,1)S(1)} %broadcast_select_fusion.7), channel_id=1, source_target_pairs={{0,1},{1,0},{2,3},{3,2},{4,5},{5,4},{6,7},{7,6},{8,9},{9,8},{10,11... | collective-permute-start | bytes 98312 | tf_op jit(solution)/shard_map/ppermute | solution.py:14
  18.6 1.7 gather_fusion.1
  20.3 0.1 broadcast_select_fusion.5
  20.3 1.9 collective-permute-start.1
  22.3 1.7 gather_fusion.2
  23.9 0.1 broadcast_select_fusion.3
  24.0 2.5 collective-permute-start.2
  26.6 1.7 gather_fusion.3
  28.3 0.1 broadcast_select_fusion.1
  28.4 0.0 copy-start.6
  28.4 7.9 %collective-permute-start.3 = (bf16[128,128]{1,0:T(8,128)(2,1)S(1)}, bf16[128,128]{1,0:T(8,128)(2,1)S(1)}, u32[]{:S(2)}, u32[]{:S(2)}) collective-permute-start(bf16[128,128]{1,0:T(8,128)(2,1)S(1)} %broadcast_select_fusion.1), channel_id=1, source_target_pairs={{0,8},{1,9},{2,10},{3,11},{4,12},{5,13},{6,14},{7,15},{8,0},{9,1},... | collective-permute-start | bytes 98312 | tf_op jit(solution)/shard_map/ppermute | solution.py:14
  36.3 5.2 %copy.15 = bf16[1152,1152]{0,1:T(8,128)(2,1)} copy(bf16[1152,1152]{1,0:T(8,128)(2,1)} %param.14) | data formatting | bytes 5308416 | tf_op args[4]
  41.6 0.1 copy.14
  41.7 0.1 broadcast_in_dim.20
  41.8 0.1 convert_element_type.59
  41.9 0.0 copy-start.3
  41.9 2.1 bitcast_multiply_fusion
  44.0 0.0 copy-start.7
  44.0 0.0 copy-start.8
  44.0 0.9 fusion.41
  45.0 0.5 fusion.2
  45.5 0.0 copy-done.1
  45.5 0.3 add_convert_fusion
  45.8 0.7 gather_fusion.4
  46.6 0.7 gather_fusion.5
  47.3 0.7 gather_fusion.6
  48.0 0.7 gather_fusion.7
  48.7 0.1 broadcast_select_fusion.6
  48.8 2.8 collective-permute-start.4
  51.5 0.1 broadcast_select_fusion.4
  51.6 2.2 collective-permute-start.5
  53.8 0.1 broadcast_select_fusion.2
  53.9 2.2 collective-permute-start.6
  56.1 0.1 broadcast_select_fusion
  56.2 0.0 copy-start.5
  56.2 3.9 %collective-permute-start.7 = (bf16[128,128]{1,0:T(8,128)(2,1)S(1)}, bf16[128,128]{1,0:T(8,128)(2,1)S(1)}, u32[]{:S(2)}, u32[]{:S(2)}) collective-permute-start(bf16[128,128]{1,0:T(8,128)(2,1)S(1)} %broadcast_select_fusion), channel_id=1, source_target_pairs={{0,8},{1,9},{2,10},{3,11},{4,12},{5,13},{6,14},{7,15},{8,0},{9,1},... | collective-permute-start | bytes 98312 | tf_op jit(solution)/shard_map/ppermute | solution.py:14
  60.1 2.7 fusion.42
  62.8 0.0 copy-start.4
  62.8 2.2 collective-permute-done.7
  65.0 0.5 fusion.3
  65.5 0.9 fusion.40
  66.4 0.2 convolution_convert_fusion
  66.7 0.9 convolution_add_fusion
  67.5 0.6 fusion.4
  68.1 3.5 collective-permute-start.8
  71.6 3.1 collective-permute-start.9
  74.7 4.0 %collective-permute-start.10 = (bf16[128,128]{1,0:T(8,128)(2,1)S(1)}, bf16[128,128]{1,0:T(8,128)(2,1)S(1)}, u32[]{:S(2)}, u32[]{:S(2)}) collective-permute-start(bf16[128,128]{1,0:T(8,128)(2,1)S(1)} %get-tuple-element.15), channel_id=1, source_target_pairs={{0,4},{1,5},{2,6},{3,7},{4,0},{5,1},{6,2},{7,3},{8,12},{9,13},{10,... | collective-permute-start | bytes 98312 | tf_op jit(solution)/shard_map/ppermute | solution.py:14
  78.7 2.7 collective-permute-start.11
  81.4 0.9 fusion.36
  82.3 1.5 scatter_custom_fusion
  83.8 1.5 scatter_custom_fusion.1
  85.3 1.5 scatter_custom_fusion.2
  86.8 0.5 collective-permute-done.11
  87.3 1.5 scatter_custom_fusion.3
  88.8 1.0 fusion.6
  89.8 0.0 all-reduce.3.cloned.1.call-update
  89.8 266.9 %all-reduce.3.cloned.1.call-done = (f32[128,128]{1,0:T(8,128)}, f32[128,128]{1,0:T(8,128)}) async-done(((f32[128,128]{1,0:T(8,128)}, f32[128,128]{1,0:T(8,128)}), (f32[128,128]{1,0:T(8,128)}, f32[128,128]{1,0:T(8,128)})) %all-reduce.3.cloned.1.call-update) | async-done | bytes 131088 | tf_op jit(solution)/shard_map/psum | solution.py:86
  356.8 1.5 copy.28
  358.3 1.5 copy.29
  (27 shorter events, 0.1 us)
Async XLA Ops:
  7.2 37.9 %copy-start = (bf16[1152,512]{1,0:T(8,128)(2,1)S(1)}, bf16[1152,512]{1,0:T(8,128)(2,1)}, u32[]{:S(2)}) copy-start(bf16[1152,512]{1,0:T(8,128)(2,1)} %param.15) | copy-start | bytes 3538948
  7.2 349.6 %all-reduce.3.cloned.1.call-start = ((), (), s32[]{:S(2)}) async-start(), calls=%async_computation | async-start | bytes 262144 | tf_op jit(solution)/shard_map/psum | solution.py:86
  9.8 35.1 %collective-permute-start = (bf16[128,128]{1,0:T(8,128)(2,1)S(1)}, bf16[128,128]{1,0:T(8,128)(2,1)S(1)}, u32[]{:S(2)}, u32[]{:S(2)}) collective-permute-start(bf16[128,128]{1,0:T(8,128)(2,1)S(1)} %broadcast_select_fusion.7), channel_id=1, source_target_pairs={{0,1},{1,0},{2,3},{3,2},{4,5},{5,4},{6,7},{7,6},{8,9},{9,8},{10,11... | collective-permute-start | bytes 98312 | tf_op jit(solution)/shard_map/ppermute | solution.py:14
  20.3 24.6 %collective-permute-start.1 = (bf16[128,128]{1,0:T(8,128)(2,1)S(1)}, bf16[128,128]{1,0:T(8,128)(2,1)S(1)}, u32[]{:S(2)}, u32[]{:S(2)}) collective-permute-start(bf16[128,128]{1,0:T(8,128)(2,1)S(1)} %broadcast_select_fusion.5), channel_id=1, source_target_pairs={{0,2},{1,3},{2,0},{3,1},{4,6},{5,7},{6,4},{7,5},{8,10},{9,11},{10,... | collective-permute-start | bytes 98312 | tf_op jit(solution)/shard_map/ppermute | solution.py:14
  24.0 21.0 %collective-permute-start.2 = (bf16[128,128]{1,0:T(8,128)(2,1)S(1)}, bf16[128,128]{1,0:T(8,128)(2,1)S(1)}, u32[]{:S(2)}, u32[]{:S(2)}) collective-permute-start(bf16[128,128]{1,0:T(8,128)(2,1)S(1)} %broadcast_select_fusion.3), channel_id=1, source_target_pairs={{0,4},{1,5},{2,6},{3,7},{4,0},{5,1},{6,2},{7,3},{8,12},{9,13},{10,... | collective-permute-start | bytes 98312 | tf_op jit(solution)/shard_map/ppermute | solution.py:14
  28.4 13.2 %copy-start.6 = (s32[18,18]{1,0:T(8,128)S(1)}, s32[18,18]{1,0:T(8,128)}, u32[]{:S(2)}) copy-start(s32[18,18]{1,0:T(8,128)} %param.16) | copy-start | bytes 3892
  28.4 16.7 %collective-permute-start.3 = (bf16[128,128]{1,0:T(8,128)(2,1)S(1)}, bf16[128,128]{1,0:T(8,128)(2,1)S(1)}, u32[]{:S(2)}, u32[]{:S(2)}) collective-permute-start(bf16[128,128]{1,0:T(8,128)(2,1)S(1)} %broadcast_select_fusion.1), channel_id=1, source_target_pairs={{0,8},{1,9},{2,10},{3,11},{4,12},{5,13},{6,14},{7,15},{8,0},{9,1},... | collective-permute-start | bytes 98312 | tf_op jit(solution)/shard_map/ppermute | solution.py:14
  41.9 2.1 copy-start.3
  44.0 1.5 copy-start.1
  44.0 0.9 copy-start.7
  44.0 1.5 copy-start.8
  48.8 14.0 %collective-permute-start.4 = (bf16[128,128]{1,0:T(8,128)(2,1)S(1)}, bf16[128,128]{1,0:T(8,128)(2,1)S(1)}, u32[]{:S(2)}, u32[]{:S(2)}) collective-permute-start(bf16[128,128]{1,0:T(8,128)(2,1)S(1)} %broadcast_select_fusion.6), channel_id=1, source_target_pairs={{0,1},{1,0},{2,3},{3,2},{4,5},{5,4},{6,7},{7,6},{8,9},{9,8},{10,11... | collective-permute-start | bytes 98312 | tf_op jit(solution)/shard_map/ppermute | solution.py:14
  51.6 11.2 %collective-permute-start.5 = (bf16[128,128]{1,0:T(8,128)(2,1)S(1)}, bf16[128,128]{1,0:T(8,128)(2,1)S(1)}, u32[]{:S(2)}, u32[]{:S(2)}) collective-permute-start(bf16[128,128]{1,0:T(8,128)(2,1)S(1)} %broadcast_select_fusion.4), channel_id=1, source_target_pairs={{0,2},{1,3},{2,0},{3,1},{4,6},{5,7},{6,4},{7,5},{8,10},{9,11},{10,... | collective-permute-start | bytes 98312 | tf_op jit(solution)/shard_map/ppermute | solution.py:14
  53.9 8.9 %collective-permute-start.6 = (bf16[128,128]{1,0:T(8,128)(2,1)S(1)}, bf16[128,128]{1,0:T(8,128)(2,1)S(1)}, u32[]{:S(2)}, u32[]{:S(2)}) collective-permute-start(bf16[128,128]{1,0:T(8,128)(2,1)S(1)} %broadcast_select_fusion.2), channel_id=1, source_target_pairs={{0,4},{1,5},{2,6},{3,7},{4,0},{5,1},{6,2},{7,3},{8,12},{9,13},{10,... | collective-permute-start | bytes 98312 | tf_op jit(solution)/shard_map/ppermute | solution.py:14
  56.2 9.2 %copy-start.5 = (bf16[128,128]{1,0:T(8,128)(2,1)S(1)}, bf16[128,128]{1,0:T(8,128)(2,1)}, u32[]{:S(2)}) copy-start(bf16[128,128]{1,0:T(8,128)(2,1)} %param.13) | copy-start | bytes 98308
  56.2 8.8 %collective-permute-start.7 = (bf16[128,128]{1,0:T(8,128)(2,1)S(1)}, bf16[128,128]{1,0:T(8,128)(2,1)S(1)}, u32[]{:S(2)}, u32[]{:S(2)}) collective-permute-start(bf16[128,128]{1,0:T(8,128)(2,1)S(1)} %broadcast_select_fusion), channel_id=1, source_target_pairs={{0,8},{1,9},{2,10},{3,11},{4,12},{5,13},{6,14},{7,15},{8,0},{9,1},... | collective-permute-start | bytes 98312 | tf_op jit(solution)/shard_map/ppermute | solution.py:14
  62.8 3.6 copy-start.4
  62.8 3.9 %copy-start.2 = (bf16[1152,1152]{0,1:T(8,128)(2,1)S(1)}, bf16[1152,1152]{0,1:T(8,128)(2,1)}, u32[]{:S(2)}) copy-start(bf16[1152,1152]{0,1:T(8,128)(2,1)} %copy-done.1) | copy-start | bytes 7962628
  68.1 14.2 %collective-permute-start.8 = (bf16[128,128]{1,0:T(8,128)(2,1)S(1)}, bf16[128,128]{1,0:T(8,128)(2,1)S(1)}, u32[]{:S(2)}, u32[]{:S(2)}) collective-permute-start(bf16[128,128]{1,0:T(8,128)(2,1)S(1)} %get-tuple-element.17), channel_id=1, source_target_pairs={{0,1},{1,0},{2,3},{3,2},{4,5},{5,4},{6,7},{7,6},{8,9},{9,8},{10,11... | collective-permute-start | bytes 98312 | tf_op jit(solution)/shard_map/ppermute | solution.py:14
  71.6 12.2 %collective-permute-start.9 = (bf16[128,128]{1,0:T(8,128)(2,1)S(1)}, bf16[128,128]{1,0:T(8,128)(2,1)S(1)}, u32[]{:S(2)}, u32[]{:S(2)}) collective-permute-start(bf16[128,128]{1,0:T(8,128)(2,1)S(1)} %get-tuple-element.16), channel_id=1, source_target_pairs={{0,2},{1,3},{2,0},{3,1},{4,6},{5,7},{6,4},{7,5},{8,10},{9,11},{10,... | collective-permute-start | bytes 98312 | tf_op jit(solution)/shard_map/ppermute | solution.py:14
  74.7 10.6 %collective-permute-start.10 = (bf16[128,128]{1,0:T(8,128)(2,1)S(1)}, bf16[128,128]{1,0:T(8,128)(2,1)S(1)}, u32[]{:S(2)}, u32[]{:S(2)}) collective-permute-start(bf16[128,128]{1,0:T(8,128)(2,1)S(1)} %get-tuple-element.15), channel_id=1, source_target_pairs={{0,4},{1,5},{2,6},{3,7},{4,0},{5,1},{6,2},{7,3},{8,12},{9,13},{10,... | collective-permute-start | bytes 98312 | tf_op jit(solution)/shard_map/ppermute | solution.py:14
  78.7 8.6 %collective-permute-start.11 = (bf16[128,128]{1,0:T(8,128)(2,1)S(1)}, bf16[128,128]{1,0:T(8,128)(2,1)S(1)}, u32[]{:S(2)}, u32[]{:S(2)}) collective-permute-start(bf16[128,128]{1,0:T(8,128)(2,1)S(1)} %get-tuple-element.14), channel_id=1, source_target_pairs={{0,8},{1,9},{2,10},{3,11},{4,12},{5,13},{6,14},{7,15},{8,0},{9,1},... | collective-permute-start | bytes 98312 | tf_op jit(solution)/shard_map/ppermute | solution.py:14
Sparse Core Ops, SparseCore 0:
  90.0 266.7 all-reduce.2
where the time goes:
time: 368 us; the launch traced here: 367 us
  waiting for transfers between devices  270 us (73%)
  starting transfers between devices  45.4 us (12%)
  local copies, waits for them, and re-layouts  18.1 us (5%)
  between operations  14.5 us (4%)
  other arithmetic  9.57 us (3%)
  matrix products  9.33 us (3%)
    psum x1, waiting for transfers between devices, local(): grad_first, grad_second = lax.psum((grad_first, grad_second), 'dom')  267 us
    ppermute x12, starting transfers between devices, swapped(): return lax.ppermute(value, axis, pairs)  45.4 us
    unnamed x21, local copies, waits for them, and re-layouts  8.26 us
  transfers between devices with their start and end apart: 13, of which 3 were waited for; matrix products, arithmetic and copies ran while one was open for 6% of the time, Pallas kernels for 0%

commit v1 on v0

v1 whole, which is shorter than its diff:
```python
import functools
import math

import jax
import jax.numpy as jnp
from jax import lax
from jax.experimental import pallas as pl
from jax.experimental.pallas import tpu as pltpu
from jax.sharding import PartitionSpec as P

MESH = pl.DeviceIdType.MESH
ROUNDS = 4
BF = jnp.bfloat16
F32 = jnp.float32


def dot(a, b):
    return jnp.dot(a, b, preferred_element_type=F32)


def dot_rows(a, b):
    return lax.dot_general(a, b, (((0,), (0,)), ((), ())), preferred_element_type=F32)


def dot_lanes(a, b):
    return lax.dot_general(a, b, (((1,), (1,)), ((), ())), preferred_element_type=F32)


def tree(values):
    while len(values) > 1:
        values = [values[i] + values[i + 1] for i in range(0, len(values), 2)]
    return values[0]


def subsets(bits):
    return [[b for j, b in enumerate(bits) if (d >> j) & 1] for d in range(1, 1 << len(bits))]


def body(
    groups, n, nodes,
    feat_h, targ_h, w1_h, w2_h, bonds_h, halo_h, mask_h, send_h,
    pred_h, g1_o, g2_o,
    feat, targ, w1, w2, bonds, halo, mask, send,
    spread, hot, inner, agg1, deriv, hid, agg2, err, err_b, pred,
    out_buf, in_buf, grads, got_z, sum_z, got_y, sum_y, got_x, full,
    load_sem, store_sem, hs_sem, hr_sem, as_sem, ar_sem,
):
    rows, width = feat.shape
    step = 384 if rows % 384 == 0 else 64
    blocks = [pl.ds(i, step) for i in range(0, rows, step)]
    hw = send.shape[1]

    def load(i, a, b):
        copy = pltpu.make_async_copy(a, b, load_sem.at[i])
        copy.start()
        return copy

    c_feat = load(0, feat_h, feat)
    c_send = load(1, send_h, send)
    c_mask = load(2, mask_h, mask)
    c_bonds = load(3, bonds_h, bonds)
    c_halo = load(4, halo_h, halo)
    c_w1 = load(5, w1_h, w1)
    c_w2 = load(6, w2_h, w2)
    c_targ = load(7, targ_h, targ)

    me = lax.axis_index("dom")
    delta = [
        (1 << b) * (1 - 2 * lax.rem(lax.div(me, 1 << b), 2)) for b in range(n.bit_length() - 1)
    ]

    def peer(bits):
        return me + sum(delta[b] for b in bits)

    zb, yb, xb = groups
    peers = [[peer(s) for s in subsets(g)] for g in groups]
    zsize = 1 << len(zb)
    chunk = width // zsize

    def zpos(device):
        return lax.rem(lax.div(device, 1 << zb[0]), zsize)

    barrier = pltpu.get_barrier_semaphore()
    count = 0
    for group in peers:
        for p in group:
            pl.semaphore_signal(barrier, inc=1, device_id=(p,), device_id_type=MESH)
            count += 1

    def remote(src, dst, ss, rs, p):
        return pltpu.make_async_remote_copy(
            src_ref=src, dst_ref=dst, send_sem=ss, recv_sem=rs, device_id=(p,), device_id_type=MESH
        )

    def exchange(k):
        copies = []
        for r in reversed(range(ROUNDS)):
            c = remote(
                out_buf.at[k, pl.ds(r * hw, hw)], in_buf.at[k, pl.ds(r * hw, hw)],
                hs_sem.at[k, r], hr_sem.at[k, r], peer([r]),
            )
            c.start()
            copies.append(c)
        return copies

    c_send.wait()
    for r in range(ROUNDS):
        spot = lax.broadcasted_iota(jnp.int32, (rows, hw), 0)
        hot[:, r * hw : (r + 1) * hw] = (spot == send[r : r + 1, :]).astype(F32).astype(BF)
    c_feat.wait()
    out_buf[0] = dot_rows(hot[...], feat[...]).astype(BF)
    pl.semaphore_wait(barrier, count)
    first = exchange(0)

    c_mask.wait()
    tiles = mask.shape[0]
    tile = rows // tiles
    col = lax.broadcasted_iota(jnp.int32, (tiles, rows), 1)
    total = jnp.zeros((tiles, rows), F32)
    for t in range(tiles):
        inside = (col >= t * tile) & (col < (t + 1) * tile)
        total = total + jnp.where(inside, mask[:, t : t + 1].astype(F32), 0.0)
    spread[...] = total
    c_bonds.wait()
    for t in range(tiles):
        part = pl.ds(t * tile, tile)
        bonds[part, :] = bonds[part, :] * spread[t : t + 1, :].astype(BF)
    for b in blocks:
        inner[b, :] = dot(bonds[b, :], feat[...])
    c_halo.wait()
    c_w1.wait()
    for c in first:
        c.wait_recv()
    for b in blocks:
        a = (inner[b, :] + dot(halo[b, :], in_buf[0])).astype(BF)
        agg1[b, :] = a
        u = dot(a, w1[...])
        s = jax.nn.sigmoid(u)
        hid[b, :] = (feat[b, :].astype(F32) + u * s).astype(BF)
        deriv[b, :] = s * (1.0 + u * (1.0 - s))

    out_buf[1] = dot_rows(hot[...], hid[...]).astype(BF)
    second = exchange(1)
    for b in blocks:
        inner[b, :] = dot(bonds[b, :], hid[...])
    c_w2.wait()
    c_targ.wait()
    for c in second:
        c.wait_recv()
    scale = 1.0 / math.sqrt(nodes)
    for b in blocks:
        a = (inner[b, :] + dot(halo[b, :], in_buf[1])).astype(BF)
        agg2[b, :] = a
        o = hid[b, :].astype(F32) + dot(a, w2[...])
        pred[b, :] = o.astype(BF)
        e = (o - targ[b, :].astype(F32)) * scale
        err[b, :] = e
        err_b[b, :] = e.astype(BF)
    c_pred = pltpu.make_async_copy(pred, pred_h, store_sem)
    c_pred.start()

    cot = dot_lanes(w2[...], err_b[...]).astype(BF)
    back = dot(cot, halo[...]).astype(BF)
    for r in range(ROUNDS):
        out_buf[2, r * hw : (r + 1) * hw, :] = back[:, r * hw : (r + 1) * hw].astype(F32).T.astype(BF)
    third = exchange(2)

    def all_of(k, phase, ref):
        return remote(ref, ref, as_sem.at[k, phase], ar_sem.at[k, phase], peers[0][0])

    def reduce_z(k):
        for i, p in enumerate(peers[0]):
            start = pl.multiple_of(zpos(p) * chunk, chunk)
            remote(
                grads.at[k, pl.ds(start, chunk)], got_z.at[k, i], as_sem.at[k, 0], ar_sem.at[k, 0], p
            ).start()

    def reduce_y(k):
        all_of(k, 0, got_z.at[k]).wait_recv()
        mine = pl.multiple_of(zpos(me) * chunk, chunk)
        own = grads[k, pl.ds(mine, chunk), :]
        sum_z[k] = tree([own] + [got_z[k, i] for i in range(len(peers[0]))])
        for i, p in enumerate(peers[1]):
            remote(sum_z.at[k], got_y.at[k, i], as_sem.at[k, 1], ar_sem.at[k, 1], p).start()

    def reduce_x(k):
        all_of(k, 1, got_y.at[k]).wait_recv()
        sum_y[k] = tree([sum_z[k]] + [got_y[k, i] for i in range(len(peers[1]))])
        for i, p in enumerate(peers[2]):
            remote(sum_y.at[k], got_x.at[k, i], as_sem.at[k, 2], ar_sem.at[k, 2], p).start()

    def gather_z(k):
        all_of(k, 2, got_x.at[k]).wait_recv()
        mine = pl.multiple_of(zpos(me) * chunk, chunk)
        here = full.at[k, pl.ds(mine, chunk)]
        full[k, pl.ds(mine, chunk), :] = tree([sum_y[k]] + [got_x[k, i] for i in range(len(peers[2]))])
        for p in peers[0]:
            remote(here, here, as_sem.at[k, 3], ar_sem.at[k, 3], p).start()

    def finish(k, out):
        all_of(k, 3, full.at[k, pl.ds(0, width - chunk)]).wait_recv()
        out[...] = full[k]
        all_of(k, 0, got_z.at[k]).wait_send()
        all_of(k, 1, got_y.at[k]).wait_send()
        all_of(k, 2, got_x.at[k]).wait_send()
        all_of(k, 3, full.at[k, pl.ds(0, width - chunk)]).wait_send()

    grads[0] = dot_rows(agg2[...], err_b[...])
    reduce_z(0)
    inner[...] = dot(cot, bonds[...]).T
    reduce_y(0)
    for c in third:
        c.wait_recv()
    pre = []
    for b in blocks:
        h = err[b, :] + inner[b, :] + dot(hot[b, :], in_buf[2])
        hid[b, :] = (h * deriv[b, :]).astype(BF)
    grads[1] = dot_rows(agg1[...], hid[...])
    reduce_z(1)
    reduce_x(0)
    reduce_y(1)
    gather_z(0)
    reduce_x(1)
    finish(0, g2_o)
    gather_z(1)
    finish(1, g1_o)
    for c in first + second + third:
        c.wait_send()
    c_pred.wait()


def make_local(n, groups):
    def local(features, targets, first_weight, second_weight, local_bonds, halo_bonds, tile_mask, send_rows):
        rows, width = features.shape
        hw = ROUNDS * send_rows.shape[1]
        zs, ys, xs = (1 << len(g) for g in groups)
        chunk = width // zs
        hbm = pl.BlockSpec(memory_space=pl.ANY)
        vmem = pl.BlockSpec(memory_space=pltpu.VMEM)
        args = (features, targets, first_weight, second_weight, local_bonds, halo_bonds, tile_mask, send_rows)
        tiles = tile_mask.shape[0]
        return pl.pallas_call(
            functools.partial(body, groups, n, rows * n),
            out_shape=(
                jax.ShapeDtypeStruct((rows, width), BF),
                jax.ShapeDtypeStruct((width, width), F32),
                jax.ShapeDtypeStruct((width, width), F32),
            ),
            in_specs=[hbm] * 8,
            out_specs=(hbm, vmem, vmem),
            scratch_shapes=[pltpu.VMEM(a.shape, a.dtype) for a in args]
            + [
                pltpu.VMEM((tiles, rows), F32),
                pltpu.VMEM((rows, hw), BF),
                pltpu.VMEM((rows, width), F32),
                pltpu.VMEM((rows, width), BF),
                pltpu.VMEM((rows, width), F32),
                pltpu.VMEM((rows, width), BF),
                pltpu.VMEM((rows, width), BF),
                pltpu.VMEM((rows, width), F32),
                pltpu.VMEM((rows, width), BF),
                pltpu.VMEM((rows, width), BF),
                pltpu.VMEM((3, hw, width), BF),
                pltpu.VMEM((3, hw, width), BF),
                pltpu.VMEM((2, width, width), F32),
                pltpu.VMEM((2, zs - 1, chunk, width), F32),
                pltpu.VMEM((2, chunk, width), F32),
                pltpu.VMEM((2, ys - 1, chunk, width), F32),
                pltpu.VMEM((2, chunk, width), F32),
                pltpu.VMEM((2, xs - 1, chunk, width), F32),
                pltpu.VMEM((2, width, width), F32),
                pltpu.SemaphoreType.DMA((8,)),
                pltpu.SemaphoreType.DMA,
                pltpu.SemaphoreType.DMA((3, ROUNDS)),
                pltpu.SemaphoreType.DMA((3, ROUNDS)),
                pltpu.SemaphoreType.DMA((2, 4)),
                pltpu.SemaphoreType.DMA((2, 4)),
            ],
            compiler_params=pltpu.CompilerParams(collective_id=0, has_side_effects=True),
            name="step",
        )(*args)

    return local


def solution(mesh):
    n = mesh.shape["dom"]
    groups = ((1, 2, 3), (4, 5, 6), (0, 7, 8)) if n == 512 else ((1, 2), (3,), (0,))
    split = P("dom", None)
    return jax.shard_map(
        make_local(n, groups),
        mesh=mesh,
        in_specs=(split, split, P(), P(), split, split, split, split),
        out_specs=(split, P(), P()),
        check_vma=False,
    )
```

time: 368 us -> 60.7 us (0.16)
  waiting for transfers between devices: 270 us -> 0 us
  Pallas kernels: 0 us -> 55.1 us
  starting transfers between devices: 45.4 us -> 0 us
  between operations: 14.5 us -> 0.64 us
  local copies, waits for them, and re-layouts: 18.1 us -> 4.64 us
  other arithmetic: 9.57 us -> 0 us
  matrix products: 9.33 us -> 0 us
    psum x1 -> x0, waiting for transfers between devices: 267 us -> none  [local(): grad_first, grad_second = lax.psum((grad_first, grad_second), 'dom')]
    pallas_call x0 -> x1, Pallas kernels: none -> 55.1 us  [local(): pl.pallas_call(functools.partial(body, groups, n, rows * n), out_shape=(j...]
    ppermute x12 -> x0, starting transfers between devices: 45.4 us -> none  [swapped(): return lax.ppermute(value, axis, pairs)]
    gather x8 -> x0, local copies, waits for them, and re-layouts: 9.46 us -> none  [the longest x4 6.62 us: fetch_inputs(): chosen = jnp.take(rows, send_rows[turn], axis=0)]
    dot_general x11 -> x0, matrix products: 9.33 us -> none  [the longest x4 3.35 us: contract_rows(): lax.dot_general(left, right, (((0,), (0,)), ((), ())), preferred_element_...]
    scatter-add x4 -> x0, other arithmetic: 5.93 us -> none  [return_grads(): total = total.at[send_rows[turn]].add(back)]
    unnamed x21 -> x3, local copies, waits for them, and re-layouts: 8.26 us -> 4.64 us
  transfers between devices with their start and end apart: 13 -> 0, of which waited for: 3 -> 0; matrix products, arithmetic and copies ran while one was open for 6% -> 0% of each run, Pallas kernels for 0% -> 0%
where the time goes in v1:
time: 60.7 us; the launch traced here: 60.4 us
  Pallas kernels  55.1 us (91%)
  local copies, waits for them, and re-layouts  4.64 us (8%)
  between operations  0.64 us (1%)
    pallas_call x1, Pallas kernels, local(): pl.pallas_call(functools.partial(body, groups, n, rows * n), out_shape=(j...  55.1 us
    unnamed x3, local copies, waits for them, and re-layouts  4.64 us

profile of v1, /device:TPU:1, one launch (start us, length us, event | category | flops | bytes accessed | tf_op | source)
XLA Modules:
  0.0 60.4 jit_solution(4227285742352069417)
XLA Ops:
  0.6 55.1 %step.1 = (bf16[1152,128]{1,0:T(8,128)(2,1)}, f32[128,128]{1,0:T(8,128)}, f32[128,128]{1,0:T(8,128)}) custom-call(bf16[1152,128]{1,0:T(8,128)(2,1)} %feat_h.1, bf16[1152,128]{1,0:T(8,128)(2,1)} %targ_h.1, bf16[128,128]{1,0:T(8,128)(2,1)} %w1_h.1, bf16[128,128]{1,0:T(8,128)(2,1)} %w2_h.1, bf16[1152,1152]{1,0:T(8,128)(2,1)} %bonds_h.1, ...), custom_call_target="tpu_custom_call" | custom-call | tf_op jit(solution)/shard_map/step/pallas_call | solution.py:242
  55.8 1.7 %copy.14 = bf16[1152,128]{1,0:T(8,128)(2,1)} copy(bf16[1152,128]{1,0:T(8,128)(2,1)} %get-tuple-element.6) | data formatting | bytes 589824
  57.5 1.5 %copy.15 = f32[128,128]{1,0:T(8,128)} copy(f32[128,128]{1,0:T(8,128)} %get-tuple-element.7) | data formatting | bytes 131072
  59.0 1.5 %copy.16 = f32[128,128]{1,0:T(8,128)} copy(f32[128,128]{1,0:T(8,128)} %get-tuple-element.8) | data formatting | bytes 131072

commit v2 on v1

v2 whole, which is shorter than its diff:
```python
import functools
import math

import jax
import jax.numpy as jnp
from jax import lax
from jax.experimental import pallas as pl
from jax.experimental.pallas import tpu as pltpu
from jax.sharding import PartitionSpec as P

MESH = pl.DeviceIdType.MESH
ROUNDS = 4
BF = jnp.bfloat16
F32 = jnp.float32
NEAR, YAXIS, ZAXIS = (0, 7, 8), (4, 5, 6), (1, 2, 3)
ORDERS = ((NEAR, YAXIS, ZAXIS), (NEAR, ZAXIS, YAXIS))
GROUP = 8


def dot(a, b):
    return jnp.dot(a, b, preferred_element_type=F32)


def tree(values):
    while len(values) > 1:
        values = [values[i] + values[i + 1] for i in range(0, len(values), 2)]
    return values[0]


def body(
    nodes,
    feat_h, targ_h, w1_h, w2_h, bonds_h, halo_h, mask_h, send_h,
    pred, grads_o,
    feat, targ, w1, w2, bonds, halo, mask, send,
    spread, hot, inner, agg1, hid, hid_far, agg2, err_t, err_bt, slope_t, slope_far_t,
    out_buf, in_buf, grads, got, part, full,
    load_sem, hs_sem, hr_sem, as_sem, ar_sem,
):
    rows, width = feat.shape
    step = 384
    blocks = [pl.ds(i, step) for i in range(0, rows, step)]
    hw = send.shape[1]
    chunk = width // GROUP

    def load(i, a, b):
        copy = pltpu.make_async_copy(a, b, load_sem.at[i])
        copy.start()
        return copy

    c_send = load(1, send_h, send)
    c_feat = load(0, feat_h, feat)
    c_mask = load(2, mask_h, mask)
    c_bonds = load(3, bonds_h, bonds)
    c_halo = load(4, halo_h, halo)
    c_w1 = load(5, w1_h, w1)
    c_w2 = load(6, w2_h, w2)
    c_targ = load(7, targ_h, targ)

    me = lax.axis_index("dom")
    delta = [(1 << b) * (1 - 2 * lax.rem(lax.div(me, 1 << b), 2)) for b in range(9)]

    def peers(bits):
        return [
            me + sum(delta[b] for j, b in enumerate(bits) if (d >> j) & 1) for d in range(1, GROUP)
        ]

    groups = {bits: peers(bits) for bits in (NEAR, YAXIS, ZAXIS)}

    def place(device):
        return pl.multiple_of((lax.rem(device, 2) + 2 * lax.div(device, 128)) * chunk, chunk)

    barrier = pltpu.get_barrier_semaphore()
    for group in groups.values():
        for p in group:
            pl.semaphore_signal(barrier, inc=1, device_id=(p,), device_id_type=MESH)

    def remote(src, dst, ss, rs, p):
        return pltpu.make_async_remote_copy(
            src_ref=src, dst_ref=dst, send_sem=ss, recv_sem=rs, device_id=(p,), device_id_type=MESH
        )

    def exchange(k):
        copies = []
        for r in reversed(range(ROUNDS)):
            c = remote(
                out_buf.at[k, pl.ds(r * hw, hw)], in_buf.at[k, pl.ds(r * hw, hw)],
                hs_sem.at[k, r], hr_sem.at[k, r], me + delta[r],
            )
            c.start()
            copies.append(c)
        return copies

    c_send.wait()
    for r in range(ROUNDS):
        wanted = jnp.broadcast_to(send[r : r + 1, :].astype(F32), (hw, hw)).T.astype(jnp.int32)
        lane = lax.broadcasted_iota(jnp.int32, (hw, hw), 1)
        for c in range(0, rows, hw):
            hot[r * hw : (r + 1) * hw, c : c + hw] = (wanted == lane + c).astype(F32).astype(BF)
    c_feat.wait()
    out_buf[0] = dot(hot[...], feat[...]).astype(BF)
    pl.semaphore_wait(barrier, 3 * (GROUP - 1))
    first = exchange(0)

    c_mask.wait()
    tiles = mask.shape[0]
    tile = rows // tiles
    col = lax.broadcasted_iota(jnp.int32, (tiles, rows), 1)
    total = jnp.zeros((tiles, rows), F32)
    for t in range(tiles):
        inside = (col >= t * tile) & (col < (t + 1) * tile)
        total = total + jnp.where(inside, mask[:, t : t + 1].astype(F32), 0.0)
    spread[...] = total
    c_bonds.wait()
    for t in range(tiles):
        here = pl.ds(t * tile, tile)
        bonds[here, :] = bonds[here, :] * spread[t : t + 1, :].astype(BF)
    for b in blocks:
        inner[b, :] = dot(bonds[b, :], feat[...])
    c_halo.wait()
    c_w1.wait()
    for c in first:
        c.wait_recv()
    for b in blocks:
        agg1[b, :] = (inner[b, :] + dot(halo[b, :], in_buf[0])).astype(BF)

    out_buf[1] = dot(hot[...], agg1[...]).astype(BF)
    second = exchange(1)

    def activate(a, x):
        u = dot(a, w1[...])
        s = jax.nn.sigmoid(u)
        return (x.astype(F32) + u * s).astype(BF), s * (1.0 + u * (1.0 - s))

    for i in range(0, rows, step):
        b = pl.ds(i, step)
        hid[b, :], slope = activate(agg1[b, :], feat[b, :])
        slope_t[:, i : i + step] = slope.T
    for b in blocks:
        inner[b, :] = dot(bonds[b, :], hid[...])
    c_w2.wait()
    c_targ.wait()
    for c in second:
        c.wait_recv()
    hid_far[...], slope = activate(in_buf[1], in_buf[0])
    slope_far_t[...] = slope.T
    scale = 1.0 / math.sqrt(nodes)
    for i in range(0, rows, step):
        b = pl.ds(i, step)
        a = (inner[b, :] + dot(halo[b, :], hid_far[...])).astype(BF)
        agg2[b, :] = a
        o = hid[b, :].astype(F32) + dot(a, w2[...])
        pred[b, :] = o.astype(BF)
        e = ((o - targ[b, :].astype(F32)) * scale).T
        err_t[:, i : i + step] = e
        err_bt[:, i : i + step] = e.astype(BF)

    def all_of(k, phase, ref):
        return remote(ref, ref, as_sem.at[k, phase], ar_sem.at[k, phase], groups[NEAR][0])

    def split(k):
        for i, p in enumerate(groups[ORDERS[k][0]]):
            remote(
                grads.at[k, pl.ds(place(p), chunk)], got.at[k, 0, i], as_sem.at[k, 0], ar_sem.at[k, 0], p
            ).start()

    def add(k, phase):
        all_of(k, phase, got.at[k, phase]).wait_recv()
        own = grads[k, pl.ds(place(me), chunk), :] if phase == 0 else part[k, phase - 1]
        return tree([own] + [got[k, phase, i] for i in range(GROUP - 1)])

    def share(k, phase):
        part[k, phase] = add(k, phase)
        for i, p in enumerate(groups[ORDERS[k][phase + 1]]):
            remote(
                part.at[k, phase], got.at[k, phase + 1, i],
                as_sem.at[k, phase + 1], ar_sem.at[k, phase + 1], p,
            ).start()

    def gather(k):
        here = full.at[k, pl.ds(place(me), chunk)]
        full[k, pl.ds(place(me), chunk), :] = add(k, 2)
        for p in groups[NEAR]:
            remote(here, here, as_sem.at[k, 3], ar_sem.at[k, 3], p).start()

    def finish(k):
        rest = full.at[k, pl.ds(0, width - chunk)]
        all_of(k, 3, rest).wait_recv()
        grads_o[k] = full[k]
        for phase in range(3):
            all_of(k, phase, got.at[k, phase]).wait_send()
        all_of(k, 3, rest).wait_send()

    grads[0] = dot(err_bt[...], agg2[...])
    split(0)
    cot = dot(w2[...], err_bt[...]).astype(BF)
    near = ((err_t[...] + dot(cot, bonds[...])) * slope_t[...]).astype(BF)
    far = (dot(cot, halo[...]) * slope_far_t[...]).astype(BF)
    grads[1] = dot(near, agg1[...]) + dot(far, in_buf[1])
    split(1)
    for phase in range(2):
        share(0, phase)
        share(1, phase)
    gather(0)
    gather(1)
    for c in first + second:
        c.wait_send()
    finish(0)
    finish(1)


def write_out(pred_i, grads_i, pred_o, g1_o, g2_o):
    pred_o[...] = pred_i[...]
    g2_o[...] = grads_i[0].T
    g1_o[...] = grads_i[1].T


def make_local(n):
    def local(features, targets, first_weight, second_weight, local_bonds, halo_bonds, tile_mask, send_rows):
        rows, width = features.shape
        hw = ROUNDS * send_rows.shape[1]
        chunk = width // GROUP
        hbm = pl.BlockSpec(memory_space=pltpu.HBM)
        vmem = pl.BlockSpec(memory_space=pltpu.VMEM)
        args = (features, targets, first_weight, second_weight, local_bonds, halo_bonds, tile_mask, send_rows)
        pred, grads = pl.pallas_call(
            functools.partial(body, rows * n),
            out_shape=(
                pltpu.VMEM((rows, width), BF),
                pltpu.VMEM((2, width, width), F32),
            ),
            in_specs=[hbm] * 8,
            out_specs=(vmem, vmem),
            scratch_shapes=[pltpu.VMEM(a.shape, a.dtype) for a in args]
            + [
                pltpu.VMEM((tile_mask.shape[0], rows), F32),
                pltpu.VMEM((hw, rows), BF),
                pltpu.VMEM((rows, width), F32),
                pltpu.VMEM((rows, width), BF),
                pltpu.VMEM((rows, width), BF),
                pltpu.VMEM((hw, width), BF),
                pltpu.VMEM((rows, width), BF),
                pltpu.VMEM((width, rows), F32),
                pltpu.VMEM((width, rows), BF),
                pltpu.VMEM((width, rows), F32),
                pltpu.VMEM((width, hw), F32),
                pltpu.VMEM((2, hw, width), BF),
                pltpu.VMEM((2, hw, width), BF),
                pltpu.VMEM((2, width, width), F32),
                pltpu.VMEM((2, 3, GROUP - 1, chunk, width), F32),
                pltpu.VMEM((2, 2, chunk, width), F32),
                pltpu.VMEM((2, width, width), F32),
                pltpu.SemaphoreType.DMA((8,)),
                pltpu.SemaphoreType.DMA((2, ROUNDS)),
                pltpu.SemaphoreType.DMA((2, ROUNDS)),
                pltpu.SemaphoreType.DMA((2, 4)),
                pltpu.SemaphoreType.DMA((2, 4)),
            ],
            compiler_params=pltpu.CompilerParams(
                collective_id=0, has_side_effects=True,
            ),
            name="step",
        )(*args)
        return pl.pallas_call(
            write_out,
            out_shape=(
                jax.ShapeDtypeStruct((rows, width), BF),
                jax.ShapeDtypeStruct((width, width), F32),
                jax.ShapeDtypeStruct((width, width), F32),
            ),
            in_specs=[vmem] * 2,
            out_specs=(vmem, vmem, vmem),
            compiler_params=pltpu.CompilerParams(vmem_limit_bytes=4 << 20),
            name="write_out",
        )(pred, grads)

    return local


def solution(mesh):
    split = P("dom", None)
    return jax.shard_map(
        make_local(mesh.shape["dom"]),
        mesh=mesh,
        in_specs=(split, split, P(), P(), split, split, split, split),
        out_specs=(split, P(), P()),
        check_vma=False,
    )
```

time: 60.7 us -> 48.1 us (0.79)
  Pallas kernels: 55.1 us -> 47.3 us
  local copies, waits for them, and re-layouts: 4.64 us -> 0 us
    pallas_call x1 -> x2, Pallas kernels: 55.1 us -> 47.3 us  [the longest x1 46.5 us: local(): pl.pallas_call(functools.partial(body, rows * n), out_shape=(pltpu.VMEM((...]
    unnamed x3 -> x0, local copies, waits for them, and re-layouts: 4.64 us -> none
where the time goes in v2:
time: 48.1 us; the launch traced here: 47.9 us
  Pallas kernels  47.3 us (98%)
  between operations  0.64 us (1%)
    pallas_call x1, Pallas kernels, local(): pl.pallas_call(functools.partial(body, rows * n), out_shape=(pltpu.VMEM((...  46.5 us

profile of v2, /device:TPU:1, one launch (start us, length us, event | category | flops | bytes accessed | tf_op | source)
XLA Modules:
  0.0 47.9 jit_solution(13924104459251390283)
XLA Ops:
  0.6 46.5 %step.1 = (bf16[1152,128]{1,0:T(8,128)(2,1)S(1)}, f32[2,128,128]{2,1,0:T(8,128)S(1)}) custom-call(bf16[1152,128]{1,0:T(8,128)(2,1)} %feat_h.1, bf16[1152,128]{1,0:T(8,128)(2,1)} %targ_h.1, bf16[128,128]{1,0:T(8,128)(2,1)} %w1_h.1, bf16[128,128]{1,0:T(8,128)(2,1)} %w2_h.1, bf16[1152,1152]{1,0:T(8,128)(2,1)} %bonds_h.1, bf16[1152,512]{1,0:T(8,128)(2,1)} %halo_h.1, ...), custom_call_target="tpu_custom_call" | custom-call | tf_op jit(solution)/shard_map/step/pallas_call | solution.py:225
  47.2 0.8 %write_out.1 = (bf16[1152,128]{1,0:T(8,128)(2,1)}, f32[128,128]{1,0:T(8,128)}, f32[128,128]{1,0:T(8,128)}) custom-call(bf16[1152,128]{1,0:T(8,128)(2,1)S(1)} %get-tuple-element.5.pred_i, f32[2,128,128]{2,1,0:T(8,128)S(1)} %get-tuple-element.6.grads_i), custom_call_target="tpu_custom_call" | custom-call | tf_op jit(solution)/shard_map/write_out/pallas_call | solution.py:263

commit v3 on v2

--- a/solution.py
+++ b/solution.py
@@ -15,6 +15,7 @@
 NEAR, YAXIS, ZAXIS = (0, 7, 8), (4, 5, 6), (1, 2, 3)
 ORDERS = ((NEAR, YAXIS, ZAXIS), (NEAR, ZAXIS, YAXIS))
 GROUP = 8
+FAR_FIRST = (4, 5, 3, 7, 6, 2, 1)
 
 
 def dot(a, b):
@@ -32,7 +33,7 @@
     feat_h, targ_h, w1_h, w2_h, bonds_h, halo_h, mask_h, send_h,
     pred, grads_o,
     feat, targ, w1, w2, bonds, halo, mask, send,
-    spread, hot, inner, agg1, hid, hid_far, agg2, err_t, err_bt, slope_t, slope_far_t,
+    spread, hot, halves, halo_sent, sent, inner, agg1, hid, hid_far, agg2, err_t, err_bt, slope_t, slope_far_t,
     out_buf, in_buf, grads, got, part, full,
     load_sem, hs_sem, hr_sem, as_sem, ar_sem,
 ):
@@ -61,7 +62,7 @@
 
     def peers(bits):
         return [
-            me + sum(delta[b] for j, b in enumerate(bits) if (d >> j) & 1) for d in range(1, GROUP)
+            me + sum(delta[b] for j, b in enumerate(bits) if (d >> j) & 1) for d in FAR_FIRST
         ]
 
     groups = {bits: peers(bits) for bits in (NEAR, YAXIS, ZAXIS)}
@@ -70,8 +71,8 @@
         return pl.multiple_of((lax.rem(device, 2) + 2 * lax.div(device, 128)) * chunk, chunk)
 
     barrier = pltpu.get_barrier_semaphore()
-    for group in groups.values():
-        for p in group:
+    for bits in (ZAXIS, YAXIS, NEAR):
+        for p in groups[bits]:
             pl.semaphore_signal(barrier, inc=1, device_id=(p,), device_id_type=MESH)
 
     def remote(src, dst, ss, rs, p):
@@ -98,8 +99,6 @@
             hot[r * hw : (r + 1) * hw, c : c + hw] = (wanted == lane + c).astype(F32).astype(BF)
     c_feat.wait()
     out_buf[0] = dot(hot[...], feat[...]).astype(BF)
-    pl.semaphore_wait(barrier, 3 * (GROUP - 1))
-    first = exchange(0)
 
     c_mask.wait()
     tiles = mask.shape[0]
@@ -114,16 +113,27 @@
     for t in range(tiles):
         here = pl.ds(t * tile, tile)
         bonds[here, :] = bonds[here, :] * spread[t : t + 1, :].astype(BF)
+    pl.semaphore_wait(barrier, 3 * (GROUP - 1))
+    first = exchange(0)
+
     for b in blocks:
-        inner[b, :] = dot(bonds[b, :], feat[...])
+        v = dot(bonds[b, :], feat[...])
+        inner[b, :] = v
+        high = v.astype(BF)
+        halves[b, :width] = high
+        halves[b, width:] = (v - high.astype(F32)).astype(BF)
     c_halo.wait()
+    halo_sent[...] = dot(hot[...], halo[...]).astype(BF)
+    both = dot(hot[...], halves[...])
+    sent[...] = both[:, :width] + both[:, width:]
     c_w1.wait()
-    for c in first:
+    last = (ROUNDS - 1) * hw
+    for c in first[1:]:
         c.wait_recv()
-    for b in blocks:
-        agg1[b, :] = (inner[b, :] + dot(halo[b, :], in_buf[0])).astype(BF)
-
-    out_buf[1] = dot(hot[...], agg1[...]).astype(BF)
+    sent[...] += dot(halo_sent[:, :last], in_buf[0, :last, :])
+    first[0].wait_recv()
+
+    out_buf[1] = (sent[...] + dot(halo_sent[:, last:], in_buf[0, last:, :])).astype(BF)
     second = exchange(1)
 
     def activate(a, x):
@@ -133,20 +143,25 @@
 
     for i in range(0, rows, step):
         b = pl.ds(i, step)
-        hid[b, :], slope = activate(agg1[b, :], feat[b, :])
+        a = (inner[b, :] + dot(halo[b, :], in_buf[0])).astype(BF)
+        agg1[b, :] = a
+        hid[b, :], slope = activate(a, feat[b, :])
         slope_t[:, i : i + step] = slope.T
-    for b in blocks:
-        inner[b, :] = dot(bonds[b, :], hid[...])
     c_w2.wait()
     c_targ.wait()
-    for c in second:
+    for c in second[1:]:
         c.wait_recv()
-    hid_far[...], slope = activate(in_buf[1], in_buf[0])
-    slope_far_t[...] = slope.T
+    hid_far[:last, :], slope = activate(in_buf[1, :last, :], in_buf[0, :last, :])
+    slope_far_t[:, :last] = slope.T
+    for b in blocks:
+        inner[b, :] = dot(bonds[b, :], hid[...]) + dot(halo[b, :last], hid_far[:last, :])
+    second[0].wait_recv()
+    hid_far[last:, :], slope = activate(in_buf[1, last:, :], in_buf[0, last:, :])
+    slope_far_t[:, last:] = slope.T
     scale = 1.0 / math.sqrt(nodes)
     for i in range(0, rows, step):
         b = pl.ds(i, step)
-        a = (inner[b, :] + dot(halo[b, :], hid_far[...])).astype(BF)
+        a = (inner[b, :] + dot(halo[b, last:], hid_far[last:, :])).astype(BF)
         agg2[b, :] = a
         o = hid[b, :].astype(F32) + dot(a, w2[...])
         pred[b, :] = o.astype(BF)
@@ -166,7 +181,7 @@
     def add(k, phase):
         all_of(k, phase, got.at[k, phase]).wait_recv()
         own = grads[k, pl.ds(place(me), chunk), :] if phase == 0 else part[k, phase - 1]
-        return tree([own] + [got[k, phase, i] for i in range(GROUP - 1)])
+        return tree([own] + [got[k, phase, FAR_FIRST.index(d)] for d in range(1, GROUP)])
 
     def share(k, phase):
         part[k, phase] = add(k, phase)
@@ -234,6 +249,9 @@
             + [
                 pltpu.VMEM((tile_mask.shape[0], rows), F32),
                 pltpu.VMEM((hw, rows), BF),
+                pltpu.VMEM((rows, 2 * width), BF),
+                pltpu.VMEM((hw, hw), BF),
+                pltpu.VMEM((hw, width), F32),
                 pltpu.VMEM((rows, width), F32),
                 pltpu.VMEM((rows, width), BF),
                 pltpu.VMEM((rows, width), BF),

time: 48.1 us -> 47 us (0.977)
  Pallas kernels: 47.3 us -> 46.3 us
    pallas_call x1, Pallas kernels: 46.5 us -> 45.5 us  [local(): pl.pallas_call(functools.partial(body, rows * n), out_shape=(pltpu.VMEM((...]
where the time goes in v3:
time: 47 us; the launch traced here: 46.9 us
  Pallas kernels  46.3 us (99%)
  between operations  0.64 us (1%)
    pallas_call x1, Pallas kernels, local(): pl.pallas_call(functools.partial(body, rows * n), out_shape=(pltpu.VMEM((...  45.5 us

profile of v3, /device:TPU:1, one launch (start us, length us, event | category | flops | bytes accessed | tf_op | source)
XLA Modules:
  0.0 46.9 jit_solution(18366351669923382283)
XLA Ops:
  0.6 45.5 %step.1 = (bf16[1152,128]{1,0:T(8,128)(2,1)S(1)}, f32[2,128,128]{2,1,0:T(8,128)S(1)}) custom-call(bf16[1152,128]{1,0:T(8,128)(2,1)} %feat_h.1, bf16[1152,128]{1,0:T(8,128)(2,1)} %targ_h.1, bf16[128,128]{1,0:T(8,128)(2,1)} %w1_h.1, bf16[128,128]{1,0:T(8,128)(2,1)} %w2_h.1, bf16[1152,1152]{1,0:T(8,128)(2,1)} %bonds_h.1, bf16[1152,512]{1,0:T(8,128)(2,1)} %halo_h.1, ...), custom_call_target="tpu_custom_call" | custom-call | tf_op jit(solution)/shard_map/step/pallas_call | solution.py:240
  46.1 0.8 %write_out.1 = (bf16[1152,128]{1,0:T(8,128)(2,1)}, f32[128,128]{1,0:T(8,128)}, f32[128,128]{1,0:T(8,128)}) custom-call(bf16[1152,128]{1,0:T(8,128)(2,1)S(1)} %get-tuple-element.5.pred_i, f32[2,128,128]{2,1,0:T(8,128)S(1)} %get-tuple-element.6.grads_i), custom_call_target="tpu_custom_call" | custom-call | tf_op jit(solution)/shard_map/write_out/pallas_call | solution.py:281

commit v4 on v3

--- a/solution.py
+++ b/solution.py
@@ -80,16 +80,13 @@
             src_ref=src, dst_ref=dst, send_sem=ss, recv_sem=rs, device_id=(p,), device_id_type=MESH
         )
 
-    def exchange(k):
-        copies = []
-        for r in reversed(range(ROUNDS)):
-            c = remote(
-                out_buf.at[k, pl.ds(r * hw, hw)], in_buf.at[k, pl.ds(r * hw, hw)],
-                hs_sem.at[k, r], hr_sem.at[k, r], me + delta[r],
-            )
-            c.start()
-            copies.append(c)
-        return copies
+    def pass_on(k, r):
+        c = remote(
+            out_buf.at[k, pl.ds(r * hw, hw)], in_buf.at[k, pl.ds(r * hw, hw)],
+            hs_sem.at[k, r], hr_sem.at[k, r], me + delta[r],
+        )
+        c.start()
+        return c
 
     c_send.wait()
     for r in range(ROUNDS):
@@ -114,7 +111,7 @@
         here = pl.ds(t * tile, tile)
         bonds[here, :] = bonds[here, :] * spread[t : t + 1, :].astype(BF)
     pl.semaphore_wait(barrier, 3 * (GROUP - 1))
-    first = exchange(0)
+    first = [pass_on(0, ROUNDS - 1)]
 
     for b in blocks:
         v = dot(bonds[b, :], feat[...])
@@ -122,6 +119,7 @@
         high = v.astype(BF)
         halves[b, :width] = high
         halves[b, width:] = (v - high.astype(F32)).astype(BF)
+    first += [pass_on(0, r) for r in reversed(range(ROUNDS - 1))]
     c_halo.wait()
     halo_sent[...] = dot(hot[...], halo[...]).astype(BF)
     both = dot(hot[...], halves[...])
@@ -133,8 +131,9 @@
     sent[...] += dot(halo_sent[:, :last], in_buf[0, :last, :])
     first[0].wait_recv()
 
-    out_buf[1] = (sent[...] + dot(halo_sent[:, last:], in_buf[0, last:, :])).astype(BF)
-    second = exchange(1)
+    out_buf[1, last:, :] = (sent[last:, :] + dot(halo_sent[last:, last:], in_buf[0, last:, :])).astype(BF)
+    second = [pass_on(1, ROUNDS - 1)]
+    out_buf[1, :last, :] = (sent[:last, :] + dot(halo_sent[:last, last:], in_buf[0, last:, :])).astype(BF)
 
     def activate(a, x):
         u = dot(a, w1[...])
@@ -147,6 +146,8 @@
         agg1[b, :] = a
         hid[b, :], slope = activate(a, feat[b, :])
         slope_t[:, i : i + step] = slope.T
+        if i == 0:
+            second += [pass_on(1, r) for r in reversed(range(ROUNDS - 1))]
     c_w2.wait()
     c_targ.wait()
     for c in second[1:]:

time: 47 us -> 47.3 us (level)
  no operation moved by 1% of the time
where the time goes in v4:
time: 47.3 us; the launch traced here: 47.2 us
  Pallas kernels  46.5 us (98%)
  between operations  0.64 us (1%)
    pallas_call x1, Pallas kernels, local(): pl.pallas_call(functools.partial(body, rows * n), out_shape=(pltpu.VMEM((...  45.7 us

profile of v4, /device:TPU:1, one launch (start us, length us, event | category | flops | bytes accessed | tf_op | source)
XLA Modules:
  0.0 47.2 jit_solution(448522587028491700)
XLA Ops:
  0.6 45.7 %step.1 = (bf16[1152,128]{1,0:T(8,128)(2,1)S(1)}, f32[2,128,128]{2,1,0:T(8,128)S(1)}) custom-call(bf16[1152,128]{1,0:T(8,128)(2,1)} %feat_h.1, bf16[1152,128]{1,0:T(8,128)(2,1)} %targ_h.1, bf16[128,128]{1,0:T(8,128)(2,1)} %w1_h.1, bf16[128,128]{1,0:T(8,128)(2,1)} %w2_h.1, bf16[1152,1152]{1,0:T(8,128)(2,1)} %bonds_h.1, bf16[1152,512]{1,0:T(8,128)(2,1)} %halo_h.1, ...), custom_call_target="tpu_custom_call" | custom-call | tf_op jit(solution)/shard_map/step/pallas_call | solution.py:241
  46.4 0.8 %write_out.1 = (bf16[1152,128]{1,0:T(8,128)(2,1)}, f32[128,128]{1,0:T(8,128)}, f32[128,128]{1,0:T(8,128)}) custom-call(bf16[1152,128]{1,0:T(8,128)(2,1)S(1)} %get-tuple-element.5.pred_i, f32[2,128,128]{2,1,0:T(8,128)S(1)} %get-tuple-element.6.grads_i), custom_call_target="tpu_custom_call" | custom-call | tf_op jit(solution)/shard_map/write_out/pallas_call | solution.py:282

commit v5 on v3

--- a/solution.py
+++ b/solution.py
@@ -13,7 +13,7 @@
 BF = jnp.bfloat16
 F32 = jnp.float32
 NEAR, YAXIS, ZAXIS = (0, 7, 8), (4, 5, 6), (1, 2, 3)
-ORDERS = ((NEAR, YAXIS, ZAXIS), (NEAR, ZAXIS, YAXIS))
+ORDERS = ((NEAR, ZAXIS, YAXIS), (NEAR, YAXIS, ZAXIS))
 GROUP = 8
 FAR_FIRST = (4, 5, 3, 7, 6, 2, 1)
 

time: 47 us -> 47.1 us (level)
  no operation moved by 1% of the time
where the time goes in v5:
time: 47.1 us; the launch traced here: 47 us
  Pallas kernels  46.4 us (99%)
  between operations  0.64 us (1%)
    pallas_call x1, Pallas kernels, local(): pl.pallas_call(functools.partial(body, rows * n), out_shape=(pltpu.VMEM((...  45.6 us

profile of v5, /device:TPU:1, one launch (start us, length us, event | category | flops | bytes accessed | tf_op | source)
XLA Modules:
  0.0 47.0 jit_solution(18334733626325377172)
XLA Ops:
  0.6 45.6 %step.1 = (bf16[1152,128]{1,0:T(8,128)(2,1)S(1)}, f32[2,128,128]{2,1,0:T(8,128)S(1)}) custom-call(bf16[1152,128]{1,0:T(8,128)(2,1)} %feat_h.1, bf16[1152,128]{1,0:T(8,128)(2,1)} %targ_h.1, bf16[128,128]{1,0:T(8,128)(2,1)} %w1_h.1, bf16[128,128]{1,0:T(8,128)(2,1)} %w2_h.1, bf16[1152,1152]{1,0:T(8,128)(2,1)} %bonds_h.1, bf16[1152,512]{1,0:T(8,128)(2,1)} %halo_h.1, ...), custom_call_target="tpu_custom_call" | custom-call | tf_op jit(solution)/shard_map/step/pallas_call | solution.py:240
  46.2 0.8 %write_out.1 = (bf16[1152,128]{1,0:T(8,128)(2,1)}, f32[128,128]{1,0:T(8,128)}, f32[128,128]{1,0:T(8,128)}) custom-call(bf16[1152,128]{1,0:T(8,128)(2,1)S(1)} %get-tuple-element.5.pred_i, f32[2,128,128]{2,1,0:T(8,128)S(1)} %get-tuple-element.6.grads_i), custom_call_target="tpu_custom_call" | custom-call | tf_op jit(solution)/shard_map/write_out/pallas_call | solution.py:281
